TPU v7x, 256 devices: a whole 4x4x8 slice. The times are simulated.
256 devices in a mesh: comp: 2 (over x_lo), ox: 16 (over x_hi, y, core), oy: 8 (over z).
Axes of the slice: x: 4 (x_hi: 2, x_lo: 2; x = x_hi * 2 + x_lo), y: 4, z: 8, core: 2. Of those that a mesh axis runs over, the one named last changes fastest.
Arguments:
- atmos_stress: float32 [2, 2359296], P(None, ('comp', 'ox', 'oy')), may hold values from -6 to 6
- route_tile: int32 [2359296, 1], P(('comp', 'ox', 'oy')), may hold values from 0 to 255; in each aligned block of 9216 rows (0 to 9215, 9216 to 18431, ...) at most 144 rows name the same one
- route_cell: int32 [2359296], P(('comp', 'ox', 'oy')), may hold values from 0 to 54674
- route_weight: float32 [2359296], P(('comp', 'ox', 'oy')), may hold values from 0.25 to 1
- velocity: float32 [2, 8, 4320, 3240], P(None, None, ('comp', 'ox'), 'oy'), may hold values from -6 to 6
- thickness: float32 [8, 4320, 3240], P(None, ('comp', 'ox'), 'oy'), may hold values from 0.5 to 2
- coriolis: float32 [4320, 3240], P(('comp', 'ox'), 'oy'), may hold values from -0.5 to 0.5
- ocean_axes: float32 [2, 3, 4320, 3240], P(None, None, ('comp', 'ox'), 'oy'), may hold values from -3 to 3
- ocean_mask: int32 [4320, 3240], P(('comp', 'ox'), 'oy'), may hold values 0 or 1
Outputs:
- new_velocity: float32 [2, 8, 4320, 3240], P(None, None, ('comp', 'ox'), 'oy')
Inputs may be any that keep to these rules, and one draw needn't show every extreme that they name: `route_tile`: tiles are numbered as devices, comp-major, then ox, then oy. Of the 9216 cells of one device, at most 144 name the same tile, and on some device exactly 144 do.
All inputs are finite; a program needn't handle non-finite values. No bound on the sum of `ocean_mask` on one device may be relied on, other than what follows from the above.
Results may differ from a plain program's by a relative error of at most 0.0003.
Values sent between devices are 32-bit elements; how exact they have to be, the bound alone decides.
A program may use at most 128 MiB of HBM per device.

v0:
```python
import math
import jax
import jax.numpy as jnp
import numpy as np
from jax import lax
from jax.sharding import PartitionSpec as P

A_ROWS = 48
A_COLS = 64
face_normal = np.array(
    [[1.0, 0, 0], [0, 1.0, 0], [-1.0, 0, 0], [0, -1.0, 0], [0, 0, 1.0], [0, 0, -1.0]]
)
face_first = np.array(
    [[0, 1.0, 0], [-1.0, 0, 0], [0, -1.0, 0], [1.0, 0, 0], [0, 1.0, 0], [0, 1.0, 0]]
)
face_second = np.array(
    [[0, 0, 1.0], [0, 0, 1.0], [0, 0, 1.0], [0, 0, 1.0], [-1.0, 0, 0], [1.0, 0, 0]]
)
viscosity = 0.2
coupling = 0.3
bottom_drag = 0.1


def extended(block, sides, width, periodic):
    for axis, dim in sides:
        count = lax.axis_size(axis)
        forward = [(i, i + 1) for i in range(count - 1)]
        if periodic:
            forward.append((count - 1, 0))
        backward = [(target, source) for source, target in forward]
        low = lax.ppermute(
            lax.slice_in_dim(block, block.shape[dim] - width, None, axis=dim), axis, forward
        )
        high = lax.ppermute(lax.slice_in_dim(block, 0, width, axis=dim), axis, backward)
        block = jnp.concatenate([low, block, high], axis=dim)
    return block


def frame_rows(face_table, face_id):
    face_numbers = jnp.arange(6, dtype=jnp.int32)
    face_hits = (face_id[None, :] == face_numbers[:, None]).astype(jnp.float32)
    return jnp.dot(
        jnp.asarray(face_table.T, dtype=jnp.float32), face_hits, precision=lax.Precision.HIGHEST
    )


def tangent(direction, radial):
    projected = direction - jnp.sum(direction * radial, axis=0, keepdims=True) * radial
    return projected / jnp.sqrt(jnp.sum(projected * projected, axis=0, keepdims=True))


def cartesian(stress, face_id, cell_row, cell_col, cube_rows, cube_cols):
    normal = frame_rows(face_normal, face_id)
    first_axis = frame_rows(face_first, face_id)
    second_axis = frame_rows(face_second, face_id)
    slant_row = jnp.tan(
        (cell_row.astype(jnp.float32) + 0.5) * (0.5 * math.pi / cube_rows) - 0.25 * math.pi
    )
    slant_col = jnp.tan(
        (cell_col.astype(jnp.float32) + 0.5) * (0.5 * math.pi / cube_cols) - 0.25 * math.pi
    )
    surface_point = normal + slant_row[None, :] * first_axis + slant_col[None, :] * second_axis
    radial = surface_point / jnp.sqrt(jnp.sum(surface_point * surface_point, axis=0, keepdims=True))
    return stress[0][None, :] * tangent(first_axis, radial) + stress[1][None, :] * tangent(
        second_axis, radial
    )


def advance(masked, east, west, north, south, thickness, coriolis, ocean_stress, sea_mask):
    laplacian = east + west + north + south - 4.0 * masked
    turning = jnp.stack([coriolis * masked[1], -coriolis * masked[0]])
    interface_depth = 0.5 * (thickness[:-1] + thickness[1:])
    inner_flux = coupling * (masked[:, :-1] - masked[:, 1:]) / interface_depth[None]
    fluxes = jnp.concatenate(
        [ocean_stress[:, None], inner_flux, bottom_drag * masked[:, -1:]], axis=1
    )
    vertical = (fluxes[:, :-1] - fluxes[:, 1:]) / thickness[None]
    return (masked + turning + viscosity * laplacian + vertical) * sea_mask


def pack_blocks(payload, target, tile_count, capacity):
    cell_count = target.shape[0]
    block_len = math.gcd(cell_count, 512)
    block_count = cell_count // block_len
    tile_numbers = jnp.arange(tile_count, dtype=jnp.int32)
    hits = (target[:, None] == tile_numbers[None, :]).astype(jnp.float32)
    hit_blocks = hits.reshape(block_count, block_len, tile_count)
    lower = (jnp.arange(block_len)[:, None] > jnp.arange(block_len)[None, :]).astype(jnp.bfloat16)
    within = jnp.einsum(
        "ij,bjt->bit", lower, hit_blocks.astype(jnp.bfloat16), preferred_element_type=jnp.float32
    )
    totals = jnp.sum(hit_blocks, axis=1)
    before = jnp.cumsum(totals, axis=0) - totals
    rank_blocks = jnp.sum((within + before[:, None, :]) * hit_blocks, axis=2)
    payload_blocks = payload.reshape(payload.shape[0], block_count, block_len).transpose(1, 0, 2)
    slot_numbers = jnp.arange(capacity, dtype=jnp.float32)

    def pack_add_block(packed, pieces):
        hit_block, rank_block, payload_block = pieces
        slot_hits = (rank_block[:, None] == slot_numbers[None, :]).astype(jnp.float32)
        spread = payload_block[:, :, None] * hit_block[None, :, :]
        return (
            packed + jnp.einsum("cgt,gs->cts", spread, slot_hits, precision=lax.Precision.HIGHEST),
            None,
        )

    start = jnp.zeros((payload.shape[0], tile_count, capacity), jnp.float32)
    packed, unused = lax.scan(pack_add_block, start, (hit_blocks, rank_blocks, payload_blocks))
    return packed


def unpack_blocks(received, tile_count, capacity, tile_width, tile_depth):
    group = 1
    while group * 2 <= tile_count and group * 2 * capacity <= 2048:
        group = group * 2
    group_count = tile_count // group
    blocks = received.reshape(4, group_count, group * capacity).transpose(1, 0, 2)
    x_numbers = jnp.arange(tile_width, dtype=jnp.int32)
    y_numbers = jnp.arange(tile_depth, dtype=jnp.int32)

    def unpack_add_block(surface, block):
        cell_number = block[3].astype(jnp.int32)
        x_offset = cell_number // tile_depth
        y_offset = cell_number % tile_depth
        x_hits = (x_offset[None, :] == x_numbers[:, None]).astype(jnp.float32)
        y_hits = (y_offset[:, None] == y_numbers[None, :]).astype(jnp.float32)
        spread = (block[:3][:, None, :] * x_hits[None]).reshape(3 * tile_width, -1)
        return (surface + jnp.dot(spread, y_hits, precision=lax.Precision.HIGHEST), None)

    start = jnp.zeros((3 * tile_width, tile_depth), jnp.float32)
    surface, unused = lax.scan(unpack_add_block, start, blocks)
    return surface.reshape(3, tile_width, tile_depth)


def shards(
    atmos_stress,
    route_tile,
    route_cell,
    route_weight,
    velocity,
    thickness,
    coriolis,
    ocean_axes,
    ocean_mask,
):
    cell_count = atmos_stress.shape[1]
    face_block = A_ROWS * A_COLS
    halves = lax.axis_size("comp")
    rows_axis = lax.axis_size("ox")
    cols_axis = lax.axis_size("oy")
    tile_count = halves * rows_axis * cols_axis
    capacity = 4 * cell_count // tile_count
    local_index = jnp.arange(cell_count, dtype=jnp.int32)
    face_id = lax.axis_index("comp") * (cell_count // face_block) + local_index // face_block
    cell_row = lax.axis_index("ox") * A_ROWS + local_index // A_COLS % A_ROWS
    cell_col = lax.axis_index("oy") * A_COLS + local_index % A_COLS
    weighted = (
        cartesian(atmos_stress, face_id, cell_row, cell_col, A_ROWS * rows_axis, A_COLS * cols_axis)
        * route_weight[None, :]
    )
    target = route_tile[:, 0]
    payload = jnp.concatenate([weighted, route_cell.astype(jnp.float32)[None, :]], axis=0)
    packed = pack_blocks(payload, target, tile_count, capacity)
    packed = packed.reshape(4, halves, rows_axis * cols_axis, capacity)
    received = lax.all_to_all(
        lax.all_to_all(packed, "comp", split_axis=1, concat_axis=1, tiled=True),
        ("ox", "oy"),
        split_axis=2,
        concat_axis=2,
        tiled=True,
    )
    tile_width = velocity.shape[2]
    tile_depth = velocity.shape[3]
    surface = unpack_blocks(received.reshape(4, -1), tile_count, capacity, tile_width, tile_depth)
    ocean_stress = jnp.sum(ocean_axes * surface[None], axis=1)
    sea_mask = ocean_mask.astype(jnp.float32)
    masked = velocity * sea_mask
    x_rims = extended(masked, ((("comp", "ox"), 2),), 1, True)
    y_rims = extended(masked, (("oy", 3),), 1, False)
    top_row = masked[:, :, :, -1]
    position = lax.axis_index("comp") * rows_axis + lax.axis_index("ox")
    whole_row = lax.all_gather(top_row, ("comp", "ox"), axis=2, tiled=True)
    mirrored = whole_row[:, :, ::-1]
    folded = lax.dynamic_slice_in_dim(mirrored, position * tile_width, tile_width, 2)
    at_fold = lax.axis_index("oy") == cols_axis - 1
    north_rim = jnp.where(at_fold, -folded, y_rims[:, :, :, -1])
    east = x_rims[:, :, 2:, :]
    west = x_rims[:, :, :-2, :]
    north = jnp.concatenate([y_rims[:, :, :, 2:-1], north_rim[:, :, :, None]], axis=3)
    south = y_rims[:, :, :, :-2]
    return advance(masked, east, west, north, south, thickness, coriolis, ocean_stress, sea_mask)


def solution(mesh):
    return jax.shard_map(
        shards,
        mesh=mesh,
        in_specs=(
            P(None, ("comp", "ox", "oy")),
            P(("comp", "ox", "oy"), None),
            P(("comp", "ox", "oy")),
            P(("comp", "ox", "oy")),
            P(None, None, ("comp", "ox"), "oy"),
            P(None, ("comp", "ox"), "oy"),
            P(("comp", "ox"), "oy"),
            P(None, None, ("comp", "ox"), "oy"),
            P(("comp", "ox"), "oy"),
        ),
        out_specs=P(None, None, ("comp", "ox"), "oy"),
        check_vma=False,
    )
```

profile of v0, /device:TPU:1, one launch (start us, length us, event | category | flops | bytes accessed | tf_op | source)
XLA Modules:
  0.0 483.1 jit_solution(10987998646943046107)
XLA Ops:
  0.5 1.5 reduce.9
  3.1 4.8 %fusion.23 = f32[18,512,256]{1,2,0:T(8,128)} fusion(s32[18,512]{1,0:T(8,128)S(1)} %eq.115), kind=kLoop, calls=%fused_computation.36 | loop fusion | flops 4718592 | bytes 9474048 | tf_op jit(solution)/shard_map/convert_element_type | solution.py:86
  9.9 3.8 fusion.22
  14.1 45.8 %while.24 = (s32[]{:T(128)}, f32[4,256,144]{1,2,0:T(8,128)S(1)}, f32[18,4,512]{2,1,0:T(4,128)S(1)}, f32[18,512,256]{1,2,0:T(8,128)}, f32[18,512]{1,0:T(8,128)S(1)}, /*index=5*/s32[]{:T(128)}, s32[]{:T(128)}) while((s32[]{:T(128)}, f32[4,256,144]{1,2,0:T(8,128)S(1)}, f32[18,4,512]{2,1,0:T(4,128)S(1)}, f32[18,512,256]{1,2,0:T(8,128)}, ...), condition=%wide.region_9.10_spmd.clone, body=%wide.region_8.9_spmd.clone.sunk | while | flops 906862592 | bytes 3831907 | solution.py:108
  60.8 3.5 all-to-all-start
  64.5 8.8 %copy.50 = f32[2,8,135,405]{2,1,0,3:T(8,128)} copy(f32[2,8,135,405]{3,1,2,0:T(8,128)} %param.20) | data formatting | bytes 6998400 | tf_op args[4]
  73.3 3.9 broadcast_multiply_fusion.1
  79.1 5.6 %collective-permute-start.3 = (f32[2,8,135,1]{2,1,0,3:T(8,128)S(1)}, f32[2,8,135,1]{2,1,0,3:T(8,128)}, u32[]{:S(2)}, u32[]{:S(2)}) collective-permute-start(f32[2,8,135,1]{2,1,0,3:T(8,128)S(1)} %get-tuple-element.195), channel_id=1, source_target_pairs={{0,1},{1,2},{2,3},{3,4},{4,5},{5,6},{6,7},{8,9},{9,10},{10,11},{11... | collective-permute-start | bytes 25928 | tf_op jit(solution)/shard_map/ppermute | solution.py:31
  84.7 4.0 fusion.75
  88.7 2.9 copy.53
  91.6 3.0 collective-permute-start
  94.6 2.7 copy.55
  97.4 1.8 add_multiply_fusion
  99.1 4.7 copy.66
  103.8 9.4 %fusion.27 = f32[2,7,135,405]{2,1,0,3:T(8,128)} fusion(f32[2,8,135,405]{2,1,0,3:T(8,128)} %copy-done, f32[7,135,405]{1,0,2:T(8,128)} %copy.66), kind=kLoop, calls=%fused_computation.41 | loop fusion | flops 2296350 | bytes 10716300 | tf_op jit(solution)/shard_map/div | solution.py:73
  116.4 15.2 %all-to-all-start.1 = ((f32[4,2,128,144]{3,1,0,2:T(2,128)}), f32[4,2,128,144]{3,1,0,2:T(2,128)S(1)}, u32[]{:S(2)}, u32[]{:S(2)}) async-start(f32[4,2,128,144]{3,1,0,2:T(2,128)} %copy.62), calls=%async_computation.1 | async-start | bytes 2097152 | tf_op jit(solution)/shard_map/all_to_all | solution.py:165
  131.5 6.5 %slice_multiply_fusion.1 = (f32[1,8,135,405]{2,1,0,3:T(8,128)}, f32[1,8,135,405]{2,1,0,3:T(8,128)}) fusion(f32[2,8,135,405]{2,1,0,3:T(8,128)} %copy-done, f32[135,405]{0,1:T(8,128)} %copy.51, f32[135,405]{0,1:T(8,128)} %copy.52), kind=kLoop, calls=%fused_computation.59 | loop fusion | flops 874800 | bytes 7435800 | tf_op jit(solution)/shard_map/mul | solution.py:71
  138.2 4.8 slice_multiply_fusion.2
  143.0 62.0 %all-gather = f32[2,8,4320,1]{1,0,3,2:T(2,128)} all-gather(f32[2,8,135,1]{1,0,3,2:T(2,128)S(1)} %copy.57), channel_id=2, replica_groups=mesh['comp'=2,'ox'=16,'oy'=8] {'comp','ox'}, dimensions={2}, use_global_device_ids=true | all-gather | bytes 285120 | tf_op jit(solution)/shard_map/all_gather | solution.py:182
  204.9 6.4 %slice.95 = f32[2,8,135,404]{2,1,0,3:T(8,128)} slice(f32[2,8,135,405]{2,1,0,3:T(8,128)} %copy-done), slice={[0:2], [0:8], [0:135], [1:405]} | slice | bytes 6981120 | tf_op jit(solution)/shard_map/slice | solution.py:189
  211.4 3.2 copy.68
  214.6 5.2 %copy.58 = f32[2,8,4320,1]{2,1,0,3:T(8,128)S(1)} copy(f32[2,8,4320,1]{1,0,3,2:T(2,128)} %all-gather) | data formatting | bytes 552960 | tf_op jit(solution)/shard_map/all_gather | solution.py:182
  219.8 2.4 reverse
  223.2 2.5 copy.54
  225.8 2.5 copy.56
  229.0 206.2 %while.25 = (s32[]{:T(128)}, f32[405,405]{1,0:T(8,128)}, f32[32,4,1152]{2,0,1:T(8,128)S(1)}, s32[]{:T(128)}, s32[]{:T(128)}, /*index=5*/s32[]{}) while((s32[]{:T(128)}, f32[405,405]{1,0:T(8,128)}, f32[32,4,1152]{2,0,1:T(8,128)S(1)}, s32[]{:T(128)}, s32[]{:T(128)}, /*index=5*/s32[]{}) %tuple.73), condition=%wide.region_11.12_spmd.clone, body=%wide.region_10.11_spmd.clone.sunk | while | flops 2269070080 | bytes 15387791 | solution.py:131
  230.9 3.7 fusion.93
  235.9 1.5 mul.395
  237.3 3.7 fusion.93
  243.8 3.7 fusion.93
  250.2 3.7 fusion.93
  256.6 3.7 fusion.93
  263.1 3.7 fusion.93
  269.5 3.7 fusion.93
  276.0 3.7 fusion.93
  282.4 3.7 fusion.93
  288.9 3.7 fusion.93
  295.3 3.7 fusion.93
  301.7 3.7 fusion.93
  308.2 3.7 fusion.93
  314.6 3.7 fusion.93
  321.1 3.7 fusion.93
  327.5 3.7 fusion.93
  333.9 3.7 fusion.93
  340.4 3.7 fusion.93
  346.8 3.7 fusion.93
  353.3 3.7 fusion.93
  359.7 3.7 fusion.93
  366.2 3.7 fusion.93
  372.6 3.7 fusion.93
  379.0 3.7 fusion.93
  385.5 3.7 fusion.93
  391.9 3.7 fusion.93
  398.4 3.7 fusion.93
  404.8 3.7 fusion.93
  411.3 3.7 fusion.93
  417.7 3.7 fusion.93
  424.1 3.7 fusion.93
  430.6 3.7 fusion.93
  435.2 2.3 mul.269
  437.5 4.1 multiply_reduce_fusion
  441.6 3.4 copy.67
  445.0 29.2 %fusion.33 = f32[2,8,135,405]{2,1,0,3:T(8,128)} fusion(f32[2,8,135,405]{2,1,0,3:T(8,128)} %copy-done, f32[2,8,135,1]{2,1,0,3:T(8,128)} %collective-permute-done.3, f32[2,8,1,405]{2,1,0,3:T(8,128)} %copy.56, f32[2,8,1,405]{2,1,0,3:T(8,128)S(1)} %copy-done.2, f32[1,8,135,405]{2,1,0,3:T(8,128)} %get-tuple-element.197, ...), kind=kLoop, calls=%fused_computation.48 | loop fusion | flops 16621200 | bytes 19962180 | tf_op jit(solution)/shard_map/mul | solution.py:78
  474.2 8.8 %copy.69 = f32[2,8,135,405]{3,1,2,0:T(8,128)} copy(f32[2,8,135,405]{2,1,0,3:T(8,128)} %fusion.33) | data formatting | bytes 6998400 | tf_op jit(solution)/shard_map/mul | solution.py:78
  (540 shorter events, 140.0 us)
Async XLA Ops:
  0.0 7.9 %copy-start.13 = (f32[3,6]{1,0:T(4,128)S(1)}, f32[3,6]{1,0:T(4,128)}, u32[]{:S(2)}) copy-start(f32[3,6]{1,0:T(4,128)} %constant.156.clone) | copy-start | bytes 220
  0.0 8.2 %copy-start.12 = (f32[3,6]{1,0:T(4,128)S(1)}, f32[3,6]{1,0:T(4,128)}, u32[]{:S(2)}) copy-start(f32[3,6]{1,0:T(4,128)} %constant.155.clone) | copy-start | bytes 220
  0.0 8.8 %copy-start.11 = (f32[3,6]{1,0:T(4,128)S(1)}, f32[3,6]{1,0:T(4,128)}, u32[]{:S(2)}) copy-start(f32[3,6]{1,0:T(4,128)} %constant.154.clone) | copy-start | bytes 220
  0.0 9.8 %copy-start.8 = (f32[2,9216]{1,0:T(2,128)S(1)}, f32[2,9216]{1,0:T(2,128)}, u32[]{:S(2)}) copy-start(f32[2,9216]{1,0:T(2,128)} %param.16) | copy-start | bytes 221188
  0.0 9.8 %copy-start.10 = (s32[9216]{0:T(1024)S(1)}, s32[9216]{0:T(1024)}, u32[]{:S(2)}) copy-start(s32[9216]{0:T(1024)} %param.18) | copy-start | bytes 110596
  9.9 3.9 copy-start.9
  14.1 50.2 %copy-start.7 = (s32[135,405]{1,0:T(8,128)S(1)}, s32[135,405]{1,0:T(8,128)}, u32[]{:S(2)}) copy-start(s32[135,405]{1,0:T(8,128)} %param.24) | copy-start | bytes 656104
  60.8 54.3 %all-to-all-start = ((f32[4,2,128,144]{2,3,0,1:T(8,128)}), f32[4,2,128,144]{2,3,0,1:T(8,128)S(1)}, u32[]{:S(2)}, u32[]{:S(2)}) async-start(f32[4,2,128,144]{2,3,0,1:T(8,128)} %copy_bitcast_fusion.1), calls=%async_computation | async-start | bytes 1179648 | tf_op jit(solution)/shard_map/all_to_all | solution.py:166
  64.5 12.7 %copy-start.3 = (f32[135,405]{0,1:T(8,128)}, f32[135,405]{0,1:T(8,128)S(1)}, u32[]{:S(2)}) copy-start(f32[135,405]{0,1:T(8,128)S(1)} %copy.49) | copy-start | bytes 656104
  77.2 11.5 %copy-start = (f32[2,8,135,405]{2,1,0,3:T(8,128)}, f32[2,8,135,405]{2,1,0,3:T(8,128)S(1)}, u32[]{:S(2)}) copy-start(f32[2,8,135,405]{2,1,0,3:T(8,128)S(1)} %broadcast_multiply_fusion.1) | copy-start | bytes 10497604
  77.9 144.6 %collective-permute-start.2 = (f32[2,8,135,1]{2,1,0,3:T(8,128)}, f32[2,8,135,1]{2,1,0,3:T(8,128)}, u32[]{:S(2)}, u32[]{:S(2)}) collective-permute-start(f32[2,8,135,1]{2,1,0,3:T(8,128)} %get-tuple-element.194), channel_id=1, source_target_pairs={{1,0},{2,1},{3,2},{4,3},{5,4},{6,5},{7,6},{9,8},{10,9},{11,10},{12... | collective-permute-start | bytes 25928 | tf_op jit(solution)/shard_map/ppermute | solution.py:34
  79.1 365.9 %collective-permute-start.3 = (f32[2,8,135,1]{2,1,0,3:T(8,128)S(1)}, f32[2,8,135,1]{2,1,0,3:T(8,128)}, u32[]{:S(2)}, u32[]{:S(2)}) collective-permute-start(f32[2,8,135,1]{2,1,0,3:T(8,128)S(1)} %get-tuple-element.195), channel_id=1, source_target_pairs={{0,1},{1,2},{2,3},{3,4},{4,5},{5,6},{6,7},{8,9},{9,10},{10,11},{11... | collective-permute-start | bytes 25928 | tf_op jit(solution)/shard_map/ppermute | solution.py:31
  88.7 8.6 %copy-start.1 = (f32[8,135,405]{2,0,1:T(8,128)S(1)}, f32[8,135,405]{2,0,1:T(8,128)}, u32[]{:S(2)}) copy-start(f32[8,135,405]{2,0,1:T(8,128)} %param.21) | copy-start | bytes 5248804
  91.6 131.6 %collective-permute-start = (f32[2,8,1,405]{3,1,2,0:T(8,128)S(1)}, f32[2,8,1,405]{3,1,2,0:T(8,128)S(1)}, u32[]{:S(2)}, u32[]{:S(2)}) collective-permute-start(f32[2,8,1,405]{3,1,2,0:T(8,128)S(1)} %copy.53), channel_id=1, source_target_pairs={{8,0},{16,8},{24,16},{32,24},{40,32},{48,40},{56,48},{64,56},{72,6... | collective-permute-start | bytes 77768 | tf_op jit(solution)/shard_map/ppermute | solution.py:34
  97.3 128.5 %collective-permute-start.1 = (f32[2,8,1,405]{3,1,2,0:T(8,128)S(1)}, f32[2,8,1,405]{3,1,2,0:T(8,128)S(1)}, u32[]{:S(2)}, u32[]{:S(2)}) collective-permute-start(f32[2,8,1,405]{3,1,2,0:T(8,128)S(1)} %copy.55), channel_id=1, source_target_pairs={{0,8},{8,16},{16,24},{24,32},{32,40},{40,48},{48,56},{56,64},{64,7... | collective-permute-start | bytes 77768 | tf_op jit(solution)/shard_map/ppermute | solution.py:31
  103.8 9.4 %copy-start.4 = (f32[135,405]{1,0:T(8,128)S(1)}, f32[135,405]{1,0:T(8,128)}, u32[]{:S(2)}) copy-start(f32[135,405]{1,0:T(8,128)} %param.22) | copy-start | bytes 656104
  116.4 111.9 %all-to-all-start.1 = ((f32[4,2,128,144]{3,1,0,2:T(2,128)}), f32[4,2,128,144]{3,1,0,2:T(2,128)S(1)}, u32[]{:S(2)}, u32[]{:S(2)}) async-start(f32[4,2,128,144]{3,1,0,2:T(2,128)} %copy.62), calls=%async_computation.1 | async-start | bytes 2097152 | tf_op jit(solution)/shard_map/all_to_all | solution.py:165
  229.1 1.8 copy-start.5
  234.6 0.9 copy-start.6
  235.5 1.8 copy-start.5
  241.1 0.9 copy-start.6
  242.0 1.8 copy-start.5
  247.5 0.9 copy-start.6
  248.4 1.8 copy-start.5
  253.9 0.9 copy-start.6
  254.8 1.8 copy-start.5
  260.4 0.9 copy-start.6
  261.3 1.8 copy-start.5
  266.8 0.9 copy-start.6
  267.7 1.8 copy-start.5
  273.3 0.9 copy-start.6
  274.2 1.8 copy-start.5
  279.7 0.9 copy-start.6
  280.6 1.8 copy-start.5
  286.1 0.9 copy-start.6
  287.0 1.8 copy-start.5
  292.6 0.9 copy-start.6
  293.5 1.8 copy-start.5
  299.0 0.9 copy-start.6
  299.9 1.8 copy-start.5
  305.5 0.9 copy-start.6
  306.4 1.8 copy-start.5
  311.9 0.9 copy-start.6
  312.8 1.8 copy-start.5
  318.4 0.9 copy-start.6
  319.3 1.8 copy-start.5
  325.7 1.8 copy-start.5
  332.1 1.8 copy-start.5
  338.6 1.8 copy-start.5
  345.0 1.8 copy-start.5
  351.5 1.8 copy-start.5
  357.9 1.8 copy-start.5
  364.4 1.8 copy-start.5
  370.8 1.8 copy-start.5
  377.2 1.8 copy-start.5
  383.7 1.8 copy-start.5
  390.1 1.8 copy-start.5
  396.6 1.8 copy-start.5
  403.0 1.8 copy-start.5
  409.4 1.8 copy-start.5
  415.9 1.8 copy-start.5
  422.3 1.8 copy-start.5
  428.8 1.8 copy-start.5
  435.2 9.8 %copy-start.2 = (f32[2,8,1,405]{2,1,0,3:T(8,128)S(1)}, f32[2,8,1,405]{2,1,0,3:T(8,128)}, u32[]{:S(2)}) copy-start(f32[2,8,1,405]{2,1,0,3:T(8,128)} %copy.54) | copy-start | bytes 77764
  (18 other events, 16.2 us)
where the time goes:
time: 486 us; the launch traced here: 483 us
  local copies, waits for them, and re-layouts  166 us (34%)
  matrix products  145 us (30%)
  other arithmetic  77.8 us (16%)
  blocking collectives  62 us (13%)
  starting transfers between devices  28.6 us (6%)
    dot_general x32, matrix products, unpack_add_block(): jnp.dot(spread, y_hits, precision=lax.Precision.HIGHEST)  119 us
    all_gather x1, blocking collectives, shards(): whole_row = lax.all_gather(top_row, ('comp', 'ox'), axis=2, tiled=True)  62 us
    mul x32, local copies, waits for them, and re-layouts, unpack_add_block(): spread = (block[:3][:, None, :] * x_hits[None]).reshape(3 * tile_width, -1)  46.6 us
    mul x1, other arithmetic, advance(): return (masked + turning + viscosity * laplacian + vertical) * sea_mask  29.2 us
    while x160, local copies, waits for them, and re-layouts  28.7 us
    dynamic_slice x54, local copies, waits for them, and re-layouts, pack_blocks(): lax.scan(pack_add_block, start, (hit_blocks, rank_blocks, payload_blocks))  23.2 us
    dot_general x18, matrix products, pack_add_block(): jnp.einsum('cgt,gs->cts', spread, slot_hits, precision=lax.Precision.HIGH...  21.4 us
    unnamed x30, local copies, waits for them, and re-layouts  16.1 us
  transfers between devices with their start and end apart: 6, of which 0 were waited for; matrix products, arithmetic and copies ran while one was open for 54% of the time, Pallas kernels for 0%

commit v1 on v0

--- a/solution.py
+++ b/solution.py
@@ -143,6 +143,11 @@
     ocean_axes,
     ocean_mask,
 ):
+
+    def targets_assign(z, a_name):
+        block_now = lax.all_gather(z, a_name)
+        return jnp.concatenate(block_now, axis=2)
+
     cell_count = atmos_stress.shape[1]
     face_block = A_ROWS * A_COLS
     halves = lax.axis_size("comp")
@@ -179,7 +184,7 @@
     y_rims = extended(masked, (("oy", 3),), 1, False)
     top_row = masked[:, :, :, -1]
     position = lax.axis_index("comp") * rows_axis + lax.axis_index("ox")
-    whole_row = lax.all_gather(top_row, ("comp", "ox"), axis=2, tiled=True)
+    whole_row = targets_assign(top_row, ("comp", "ox"))
     mirrored = whole_row[:, :, ::-1]
     folded = lax.dynamic_slice_in_dim(mirrored, position * tile_width, tile_width, 2)
     at_fold = lax.axis_index("oy") == cols_axis - 1

time: 486 us -> 466 us (0.959)
  blocking collectives: 62 us -> 47.3 us
  local copies, waits for them, and re-layouts: 166 us -> 161 us
    all_gather x1, blocking collectives: 62 us -> 47.3 us  [targets_assign(): block_now = lax.all_gather(z, a_name)]
    all_gather x1 -> x0, local copies, waits for them, and re-layouts: 5.21 us -> none  [shards(): whole_row = lax.all_gather(top_row, ('comp', 'ox'), axis=2, tiled=True)]
  transfers between devices with their start and end apart: 6 -> 6, of which waited for: 0 -> 0; matrix products, arithmetic and copies ran while one was open for 54% -> 56% of each run, Pallas kernels for 0% -> 0%
where the time goes in v1:
time: 466 us; the launch traced here: 464 us
  local copies, waits for them, and re-layouts  161 us (35%)
  matrix products  145 us (31%)
  other arithmetic  77.8 us (17%)
  blocking collectives  47.3 us (10%)
  starting transfers between devices  28.6 us (6%)
    dot_general x32, matrix products, unpack_add_block(): jnp.dot(spread, y_hits, precision=lax.Precision.HIGHEST)  119 us
    all_gather x1, blocking collectives, targets_assign(): block_now = lax.all_gather(z, a_name)  47.3 us
    mul x32, local copies, waits for them, and re-layouts, unpack_add_block(): spread = (block[:3][:, None, :] * x_hits[None]).reshape(3 * tile_width, -1)  46.6 us
    mul x1, other arithmetic, advance(): return (masked + turning + viscosity * laplacian + vertical) * sea_mask  29.3 us
    while x160, local copies, waits for them, and re-layouts  28.3 us
    dynamic_slice x54, local copies, waits for them, and re-layouts, pack_blocks(): lax.scan(pack_add_block, start, (hit_blocks, rank_blocks, payload_blocks))  23.2 us
    dot_general x18, matrix products, pack_add_block(): jnp.einsum('cgt,gs->cts', spread, slot_hits, precision=lax.Precision.HIGH...  21.4 us
    unnamed x30, local copies, waits for them, and re-layouts  16.1 us
  transfers between devices with their start and end apart: 6, of which 0 were waited for; matrix products, arithmetic and copies ran while one was open for 56% of the time, Pallas kernels for 0%

profile of v1, /device:TPU:1, one launch (start us, length us, event | category | flops | bytes accessed | tf_op | source)
XLA Modules:
  0.0 463.5 jit_solution(1577804663145840517)
XLA Ops:
  0.5 1.5 reduce.9
  3.1 4.8 %fusion.23 = f32[18,512,256]{1,2,0:T(8,128)} fusion(s32[18,512]{1,0:T(8,128)S(1)} %eq.115), kind=kLoop, calls=%fused_computation.36 | loop fusion | flops 4718592 | bytes 9474048 | tf_op jit(solution)/shard_map/convert_element_type | solution.py:86
  9.9 3.8 fusion.22
  14.1 45.8 %while.24 = (s32[]{:T(128)}, f32[4,256,144]{1,2,0:T(8,128)S(1)}, f32[18,4,512]{2,1,0:T(4,128)S(1)}, f32[18,512,256]{1,2,0:T(8,128)}, f32[18,512]{1,0:T(8,128)S(1)}, /*index=5*/s32[]{:T(128)}, s32[]{:T(128)}) while((s32[]{:T(128)}, f32[4,256,144]{1,2,0:T(8,128)S(1)}, f32[18,4,512]{2,1,0:T(4,128)S(1)}, f32[18,512,256]{1,2,0:T(8,128)}, ...), condition=%wide.region_9.10_spmd.clone, body=%wide.region_8.9_spmd.clone.sunk | while | flops 906862592 | bytes 3831907 | solution.py:108
  60.8 3.5 all-to-all-start
  64.5 8.8 %copy.51 = f32[2,8,135,405]{2,1,0,3:T(8,128)} copy(f32[2,8,135,405]{3,1,2,0:T(8,128)} %param.20) | data formatting | bytes 6998400 | tf_op args[4]
  73.3 3.9 broadcast_multiply_fusion.1
  78.5 5.0 %collective-permute-start.3 = (f32[2,8,135,1]{2,1,0,3:T(8,128)S(1)}, f32[2,8,135,1]{2,1,0,3:T(8,128)S(1)}, u32[]{:S(2)}, u32[]{:S(2)}) collective-permute-start(f32[2,8,135,1]{2,1,0,3:T(8,128)S(1)} %get-tuple-element.196), channel_id=1, source_target_pairs={{0,1},{1,2},{2,3},{3,4},{4,5},{5,6},{6,7},{8,9},{9,10},{10,11},{11... | collective-permute-start | bytes 25928 | tf_op jit(solution)/shard_map/ppermute | solution.py:31
  83.5 4.0 fusion.74
  87.5 2.9 copy.54
  90.4 3.0 collective-permute-start
  93.4 2.7 copy.56
  96.2 1.8 add_multiply_fusion
  97.9 4.7 %copy.67 = f32[7,135,405]{1,0,2:T(8,128)} copy(f32[7,135,405]{2,0,1:T(8,128)} %add_multiply_fusion) | data formatting | bytes 3061800 | tf_op jit(solution)/shard_map/mul | solution.py:72
  102.6 9.4 %fusion.27 = f32[2,7,135,405]{2,1,0,3:T(8,128)} fusion(f32[2,8,135,405]{2,1,0,3:T(8,128)} %copy-done, f32[7,135,405]{1,0,2:T(8,128)} %copy.67), kind=kLoop, calls=%fused_computation.41 | loop fusion | flops 2296350 | bytes 10716300 | tf_op jit(solution)/shard_map/div | solution.py:73
  115.2 15.7 %all-to-all-start.1 = ((f32[4,2,128,144]{3,1,0,2:T(2,128)}), f32[4,2,128,144]{3,1,0,2:T(2,128)S(1)}, u32[]{:S(2)}, u32[]{:S(2)}) async-start(f32[4,2,128,144]{3,1,0,2:T(2,128)} %copy.63), calls=%async_computation.1 | async-start | bytes 2097152 | tf_op jit(solution)/shard_map/all_to_all | solution.py:170
  130.9 6.5 %slice_multiply_fusion.1 = (f32[1,8,135,405]{2,1,0,3:T(8,128)}, f32[1,8,135,405]{2,1,0,3:T(8,128)}) fusion(f32[2,8,135,405]{2,1,0,3:T(8,128)} %copy-done, f32[135,405]{0,1:T(8,128)} %copy.52, f32[135,405]{0,1:T(8,128)} %copy.53), kind=kLoop, calls=%fused_computation.59 | loop fusion | flops 874800 | bytes 7435800 | tf_op jit(solution)/shard_map/mul | solution.py:71
  137.4 4.8 %slice_multiply_fusion.2 = f32[2,1,135,405]{2,1,0,3:T(1,128)} fusion(f32[2,8,135,405]{2,1,0,3:T(8,128)} %copy-done), kind=kLoop, calls=%fused_computation.65 | loop fusion | flops 109350 | bytes 874800 | tf_op jit(solution)/shard_map/mul | solution.py:75
  142.2 47.3 %all-gather = f32[64,8,135,1]{2,1,3,0:T(8,128)} all-gather(f32[2,8,135,1]{2,1,3,0:T(8,128)S(1)} %get-tuple-element.194), channel_id=2, replica_groups=mesh['comp'=2,'ox'=16,'oy'=8] {'comp','ox'}, dimensions={0}, use_global_device_ids=true | all-gather | bytes 285120 | tf_op jit(solution)/shard_map/all_gather | solution.py:148
  189.4 6.4 %slice.95 = f32[2,8,135,404]{2,1,0,3:T(8,128)} slice(f32[2,8,135,405]{2,1,0,3:T(8,128)} %copy-done), slice={[0:2], [0:8], [0:135], [1:405]} | slice | bytes 6981120 | tf_op jit(solution)/shard_map/slice | solution.py:194
  195.9 3.2 copy.69
  200.7 2.4 reverse
  204.1 2.5 copy.55
  206.7 2.5 copy.57
  209.9 205.6 %while.25 = (s32[]{:T(128)}, f32[405,405]{1,0:T(8,128)}, f32[32,4,1152]{2,0,1:T(8,128)S(1)}, s32[]{:T(128)}, s32[]{:T(128)}, /*index=5*/s32[]{}) while((s32[]{:T(128)}, f32[405,405]{1,0:T(8,128)}, f32[32,4,1152]{2,0,1:T(8,128)S(1)}, s32[]{:T(128)}, s32[]{:T(128)}, /*index=5*/s32[]{}) %tuple.74), condition=%wide.region_11.12_spmd.clone, body=%wide.region_10.11_spmd.clone.sunk | while | flops 2269070080 | bytes 15387791 | solution.py:131
  211.8 3.7 fusion.92
  218.2 3.7 fusion.92
  223.2 1.5 mul.395
  224.6 3.7 fusion.92
  231.1 3.7 fusion.92
  237.5 3.7 fusion.92
  243.9 3.7 fusion.92
  250.3 3.7 fusion.92
  256.8 3.7 fusion.92
  261.7 1.5 mul.395
  263.2 3.7 fusion.92
  269.6 3.7 fusion.92
  276.0 3.7 fusion.92
  282.5 3.7 fusion.92
  288.9 3.7 fusion.92
  295.3 3.7 fusion.92
  301.7 3.7 fusion.92
  308.2 3.7 fusion.92
  314.6 3.7 fusion.92
  321.0 3.7 fusion.92
  327.4 3.7 fusion.92
  333.9 3.7 fusion.92
  340.3 3.7 fusion.92
  346.7 3.7 fusion.92
  353.1 3.7 fusion.92
  359.6 3.7 fusion.92
  366.0 3.7 fusion.92
  372.4 3.7 fusion.92
  378.8 3.7 fusion.92
  385.3 3.7 fusion.92
  391.7 3.7 fusion.92
  398.1 3.7 fusion.92
  404.5 3.7 fusion.92
  411.0 3.7 fusion.92
  415.6 2.3 mul.269
  417.9 4.1 multiply_reduce_fusion
  421.9 3.4 copy.68
  425.4 29.3 %fusion.33 = f32[2,8,135,405]{2,1,0,3:T(8,128)} fusion(f32[2,8,135,405]{2,1,0,3:T(8,128)} %copy-done, f32[2,8,135,1]{2,1,0,3:T(8,128)S(1)} %collective-permute-done.3, f32[2,8,1,405]{2,1,0,3:T(8,128)} %copy.57, f32[2,8,1,405]{2,1,0,3:T(8,128)S(1)} %copy-done.2, f32[1,8,135,405]{2,1,0,3:T(8,128)} %get-tuple-element.198, ...), kind=kLoop, calls=%fused_computation.48 | loop fusion | flops 16621200 | bytes 19962180 | tf_op jit(solution)/shard_map/mul | solution.py:78
  454.7 8.8 %copy.70 = f32[2,8,135,405]{3,1,2,0:T(8,128)} copy(f32[2,8,135,405]{2,1,0,3:T(8,128)} %fusion.33) | data formatting | bytes 6998400 | tf_op jit(solution)/shard_map/mul | solution.py:78
  (540 shorter events, 139.0 us)
Async XLA Ops:
  0.0 7.9 %copy-start.13 = (f32[3,6]{1,0:T(4,128)S(1)}, f32[3,6]{1,0:T(4,128)}, u32[]{:S(2)}) copy-start(f32[3,6]{1,0:T(4,128)} %constant.156.clone) | copy-start | bytes 220
  0.0 8.2 %copy-start.12 = (f32[3,6]{1,0:T(4,128)S(1)}, f32[3,6]{1,0:T(4,128)}, u32[]{:S(2)}) copy-start(f32[3,6]{1,0:T(4,128)} %constant.155.clone) | copy-start | bytes 220
  0.0 8.8 %copy-start.11 = (f32[3,6]{1,0:T(4,128)S(1)}, f32[3,6]{1,0:T(4,128)}, u32[]{:S(2)}) copy-start(f32[3,6]{1,0:T(4,128)} %constant.154.clone) | copy-start | bytes 220
  0.0 9.8 %copy-start.8 = (f32[2,9216]{1,0:T(2,128)S(1)}, f32[2,9216]{1,0:T(2,128)}, u32[]{:S(2)}) copy-start(f32[2,9216]{1,0:T(2,128)} %param.16) | copy-start | bytes 221188
  0.0 9.8 %copy-start.10 = (s32[9216]{0:T(1024)S(1)}, s32[9216]{0:T(1024)}, u32[]{:S(2)}) copy-start(s32[9216]{0:T(1024)} %param.18) | copy-start | bytes 110596
  9.9 3.9 copy-start.9
  14.1 50.2 %copy-start.7 = (s32[135,405]{1,0:T(8,128)S(1)}, s32[135,405]{1,0:T(8,128)}, u32[]{:S(2)}) copy-start(s32[135,405]{1,0:T(8,128)} %param.24) | copy-start | bytes 656104
  60.8 53.1 %all-to-all-start = ((f32[4,2,128,144]{2,3,0,1:T(8,128)}), f32[4,2,128,144]{2,3,0,1:T(8,128)S(1)}, u32[]{:S(2)}, u32[]{:S(2)}) async-start(f32[4,2,128,144]{2,3,0,1:T(8,128)} %copy_bitcast_fusion.1), calls=%async_computation | async-start | bytes 1179648 | tf_op jit(solution)/shard_map/all_to_all | solution.py:171
  64.5 12.7 %copy-start.3 = (f32[135,405]{0,1:T(8,128)}, f32[135,405]{0,1:T(8,128)S(1)}, u32[]{:S(2)}) copy-start(f32[135,405]{0,1:T(8,128)S(1)} %copy.50) | copy-start | bytes 656104
  77.2 10.3 %copy-start = (f32[2,8,135,405]{2,1,0,3:T(8,128)}, f32[2,8,135,405]{2,1,0,3:T(8,128)S(1)}, u32[]{:S(2)}) copy-start(f32[2,8,135,405]{2,1,0,3:T(8,128)S(1)} %broadcast_multiply_fusion.1) | copy-start | bytes 10497604
  77.2 126.1 %collective-permute-start.2 = (f32[2,8,135,1]{2,1,0,3:T(8,128)S(1)}, f32[2,8,135,1]{2,1,0,3:T(8,128)}, u32[]{:S(2)}, u32[]{:S(2)}) collective-permute-start(f32[2,8,135,1]{2,1,0,3:T(8,128)S(1)} %get-tuple-element.195), channel_id=1, source_target_pairs={{1,0},{2,1},{3,2},{4,3},{5,4},{6,5},{7,6},{9,8},{10,9},{11,10},{12... | collective-permute-start | bytes 25928 | tf_op jit(solution)/shard_map/ppermute | solution.py:34
  78.5 346.8 %collective-permute-start.3 = (f32[2,8,135,1]{2,1,0,3:T(8,128)S(1)}, f32[2,8,135,1]{2,1,0,3:T(8,128)S(1)}, u32[]{:S(2)}, u32[]{:S(2)}) collective-permute-start(f32[2,8,135,1]{2,1,0,3:T(8,128)S(1)} %get-tuple-element.196), channel_id=1, source_target_pairs={{0,1},{1,2},{2,3},{3,4},{4,5},{5,6},{6,7},{8,9},{9,10},{10,11},{11... | collective-permute-start | bytes 25928 | tf_op jit(solution)/shard_map/ppermute | solution.py:31
  87.5 8.6 %copy-start.1 = (f32[8,135,405]{2,0,1:T(8,128)S(1)}, f32[8,135,405]{2,0,1:T(8,128)}, u32[]{:S(2)}) copy-start(f32[8,135,405]{2,0,1:T(8,128)} %param.21) | copy-start | bytes 5248804
  90.4 113.7 %collective-permute-start = (f32[2,8,1,405]{3,1,2,0:T(8,128)S(1)}, f32[2,8,1,405]{3,1,2,0:T(8,128)S(1)}, u32[]{:S(2)}, u32[]{:S(2)}) collective-permute-start(f32[2,8,1,405]{3,1,2,0:T(8,128)S(1)} %copy.54), channel_id=1, source_target_pairs={{8,0},{16,8},{24,16},{32,24},{40,32},{48,40},{56,48},{64,56},{72,6... | collective-permute-start | bytes 77768 | tf_op jit(solution)/shard_map/ppermute | solution.py:34
  96.1 110.6 %collective-permute-start.1 = (f32[2,8,1,405]{3,1,2,0:T(8,128)S(1)}, f32[2,8,1,405]{3,1,2,0:T(8,128)S(1)}, u32[]{:S(2)}, u32[]{:S(2)}) collective-permute-start(f32[2,8,1,405]{3,1,2,0:T(8,128)S(1)} %copy.56), channel_id=1, source_target_pairs={{0,8},{8,16},{16,24},{24,32},{32,40},{40,48},{48,56},{56,64},{64,7... | collective-permute-start | bytes 77768 | tf_op jit(solution)/shard_map/ppermute | solution.py:31
  102.6 9.4 %copy-start.4 = (f32[135,405]{1,0:T(8,128)S(1)}, f32[135,405]{1,0:T(8,128)}, u32[]{:S(2)}) copy-start(f32[135,405]{1,0:T(8,128)} %param.22) | copy-start | bytes 656104
  115.2 94.0 %all-to-all-start.1 = ((f32[4,2,128,144]{3,1,0,2:T(2,128)}), f32[4,2,128,144]{3,1,0,2:T(2,128)S(1)}, u32[]{:S(2)}, u32[]{:S(2)}) async-start(f32[4,2,128,144]{3,1,0,2:T(2,128)} %copy.63), calls=%async_computation.1 | async-start | bytes 2097152 | tf_op jit(solution)/shard_map/all_to_all | solution.py:170
  210.0 1.8 copy-start.5
  215.5 0.9 copy-start.6
  216.4 1.8 copy-start.5
  221.9 0.9 copy-start.6
  222.8 1.8 copy-start.5
  228.4 0.9 copy-start.6
  229.3 1.8 copy-start.5
  234.8 0.9 copy-start.6
  235.7 1.8 copy-start.5
  242.1 1.8 copy-start.5
  247.6 0.9 copy-start.6
  248.5 1.8 copy-start.5
  254.1 0.9 copy-start.6
  255.0 1.8 copy-start.5
  260.5 0.9 copy-start.6
  261.4 1.8 copy-start.5
  266.9 0.9 copy-start.6
  267.8 1.8 copy-start.5
  273.3 0.9 copy-start.6
  274.2 1.8 copy-start.5
  280.7 1.8 copy-start.5
  286.2 0.9 copy-start.6
  287.1 1.8 copy-start.5
  292.6 0.9 copy-start.6
  293.5 1.8 copy-start.5
  299.0 0.9 copy-start.6
  299.9 1.8 copy-start.5
  305.5 0.9 copy-start.6
  306.4 1.8 copy-start.5
  311.9 0.9 copy-start.6
  312.8 1.8 copy-start.5
  319.2 1.8 copy-start.5
  325.6 1.8 copy-start.5
  332.1 1.8 copy-start.5
  338.5 1.8 copy-start.5
  344.9 1.8 copy-start.5
  351.3 1.8 copy-start.5
  357.8 1.8 copy-start.5
  364.2 1.8 copy-start.5
  370.6 1.8 copy-start.5
  377.0 1.8 copy-start.5
  383.5 1.8 copy-start.5
  389.9 1.8 copy-start.5
  396.3 1.8 copy-start.5
  402.7 1.8 copy-start.5
  409.2 1.8 copy-start.5
  415.6 9.8 %copy-start.2 = (f32[2,8,1,405]{2,1,0,3:T(8,128)S(1)}, f32[2,8,1,405]{2,1,0,3:T(8,128)}, u32[]{:S(2)}) copy-start(f32[2,8,1,405]{2,1,0,3:T(8,128)} %copy.55) | copy-start | bytes 77764
  (18 other events, 15.9 us)
